TPU v7x, 32 devices: a whole 2x2x4 slice. The times are simulated.
32 devices in a mesh: blk: 16 (over z, y, x), grp: 2 (over core).
Axes of the slice: x: 2, y: 2, z: 4, core: 2. Of those that a mesh axis runs over, the one named last changes fastest.
Arguments:
- schur_blocks: bfloat16 [64, 1024, 1024], P(('blk', 'grp')), may hold values from -1 to 5, as said below
- residual: float32 [64, 1024, 128], P(('blk', 'grp')), may hold values from -200 to 200
- direction: float32 [64, 1024, 128], P(('blk', 'grp')), may hold values from -200 to 200
- corner_map: int32 [64, 24], P(('blk', 'grp')), may hold values from 0 to 511
- panel_order: int32 [8], replicated, may hold values from 0 to 7, each once
- coarse_factor: float32 [8, 8, 1024, 1024], P(None, None, 'blk'), may hold values from -0.0625 to 0.0625
- block_inverses: float32 [8, 1024, 1024], P(None, 'blk'), may hold values from -0.1875 to 0.1875
Outputs:
- residual_next: float32 [64, 1024, 128], P(('blk', 'grp'))
- direction_next: float32 [64, 1024, 128], P(('blk', 'grp'))
Inputs may be any that keep to these rules, and one draw needn't show every extreme that they name: `schur_blocks`: each subdomain's block is symmetric positive definite. `panel_order`: each coarse block appears once.
All inputs are finite; a program needn't handle non-finite values.
Results may differ from a plain program's by a relative error of at most 0.0048.
Values sent between devices are 32-bit elements; how exact they have to be, the bound alone decides.
No kernel may reach another device: no remote copies, remote signals or barrier semaphores. Data moves between devices by JAX's collectives and lax.ppermute only.
A program may use at most 64 MiB of HBM per device.

v0:
```python
import jax
import jax.numpy as jnp
from jax import lax
from jax.sharding import PartitionSpec as P

PANELS = 8
precise = lax.Precision.HIGHEST


def squares(residual):
    return lax.psum(jnp.sum(residual * residual, axis=(0, 1)), ("blk", "grp"))


def solve(coarse, panel_order, coarse_factor, block_inverses):
    pending = jnp.zeros_like(coarse)
    solved = jnp.zeros_like(coarse)
    for position in range(PANELS):
        current = panel_order[position]
        target = lax.dynamic_index_in_dim(coarse - pending, current, 0, keepdims=False)
        inverse = lax.dynamic_index_in_dim(block_inverses, current, 0, keepdims=False)
        block_value = jnp.dot(
            inverse,
            lax.all_gather(target, "blk", axis=0, tiled=True),
            precision=precise,
            preferred_element_type=jnp.float32,
        )
        solved = lax.dynamic_update_index_in_dim(solved, block_value, current, 0)
        if position + 1 < PANELS:
            coupling = lax.dynamic_index_in_dim(coarse_factor, current, 1, keepdims=False)
            pending = pending + jnp.einsum(
                "aic,cv->aiv",
                coupling,
                lax.all_gather(block_value, "blk", axis=0, tiled=True),
                precision=precise,
            )
    return solved


def local(
    schur_blocks, residual, direction, corner_map, panel_order, coarse_factor, block_inverses
):
    panels = block_inverses.shape[0]
    rows_b = block_inverses.shape[1]
    sub_count = schur_blocks.shape[0]
    corners = corner_map.shape[1]
    columns_iota = lax.broadcasted_iota(jnp.int32, (sub_count, corners, panels * rows_b), 2)
    placing = (corner_map[:, :, None] == columns_iota).astype(jnp.float32)
    norm_now = squares(residual)
    applied = jnp.einsum(
        "sij,sjv->siv",
        schur_blocks,
        direction.astype(jnp.bfloat16),
        preferred_element_type=jnp.float32,
    )
    curvature = lax.psum(jnp.sum(direction * applied, axis=(0, 1)), ("blk", "grp"))
    step_size = norm_now / curvature
    residual = residual - step_size * applied
    norm_next = squares(residual)
    corner_part = jnp.einsum("scm,scv->mv", placing, residual[:, :corners, :], precision=precise)
    corner_part = corner_part.reshape(panels, rows_b, -1)
    coarse_part = lax.psum(corner_part, "grp")
    solved = solve(coarse_part, panel_order, coarse_factor, block_inverses)
    flat_solved = solved.reshape(panels * rows_b, -1)
    correction = jnp.einsum("scm,mv->scv", placing, flat_solved, precision=precise)
    corrected = jnp.concatenate(
        [residual[:, :corners, :] + correction, residual[:, corners:, :]], axis=1
    )
    direction = corrected + norm_next / norm_now * direction
    return (residual, direction)


def solution(mesh):
    in_specs = (
        P(("blk", "grp"), None, None),
        P(("blk", "grp"), None, None),
        P(("blk", "grp"), None, None),
        P(("blk", "grp"), None),
        P(),
        P(None, None, "blk", None),
        P(None, "blk", None),
    )
    out_specs = (P(("blk", "grp"), None, None), P(("blk", "grp"), None, None))
    return jax.shard_map(local, mesh=mesh, in_specs=in_specs, out_specs=out_specs, check_vma=False)
```

profile of v0, /device:TPU:0, one launch (start us, length us, event | category | flops | bytes accessed | tf_op | source)
XLA Modules:
  0.0 743.4 jit_solution(7819238958384494164)
XLA Ops:
  7.2 0.0 copy-start
  7.2 0.0 all-reduce.3.cloned.1.call-start
  7.2 1.6 multiply_reduce_fusion.2
  8.9 5.0 multiply_reduce_fusion.1
  13.9 0.0 copy-start.7
  13.9 0.0 copy-start.6
  13.9 41.9 %all-reduce = (f32[128]{0:T(128)S(1)}, f32[128]{0:T(128)S(1)}) all-reduce(f32[128]{0:T(128)S(1)} %multiply_reduce_fusion.2, f32[128]{0:T(128)S(1)} %get-tuple-element.14), channel_id=1, replica_groups=mesh['blk'=16,'grp'=2] {'blk','grp'}, use_global_device_ids=true, to_apply=%region_1.0 | all-reduce | flops 256 | bytes 2048 | tf_op jit(solution)/shard_map/psum | solution.py:11
  55.8 1.8 multiply_reduce_fusion
  57.6 0.0 copy-start.2
  57.7 0.0 copy-done.7
  57.7 1.2 fusion.77
  58.8 0.0 all-reduce.3.cloned.1.call-update
  58.9 0.0 copy-done.6
  58.9 0.7 fusion.96
  69.5 1.0 slice.42
  70.6 40.0 %psum.31 = f32[128]{0:T(128)S(1)} all-reduce(f32[128]{0:T(128)S(1)} %get-tuple-element.4), channel_id=1, replica_groups=mesh['blk'=16,'grp'=2] {'blk','grp'}, use_global_device_ids=true, to_apply=%region_6.0 | all-reduce | flops 128 | bytes 1024 | tf_op jit(solution)/shard_map/psum | solution.py:11
  115.6 0.0 all-reduce.3.cloned.1.call-done
  115.7 0.8 constant_dynamic-slice_fusion
  116.4 43.7 %all-gather = f32[1,1024,128]{2,1,0:T(8,128)S(1)} all-gather(f32[1,64,128]{2,1,0:T(8,128)S(1)} %constant_dynamic-slice_fusion), channel_id=2, replica_groups=mesh['blk'=16,'grp'=2] {'blk'}, dimensions={1}, use_global_device_ids=true | all-gather | bytes 557056 | tf_op jit(solution)/shard_map/all_gather | solution.py:23
  160.2 0.0 copy-start.5
  160.2 0.0 copy-done
  160.2 0.0 copy-start.1
  160.2 0.5 bitcast_dynamic-update-slice_fusion.6
  160.7 38.5 %all_gather.46 = f32[1024,128]{1,0:T(8,128)S(1)} all-gather(f32[64,128]{1,0:T(8,128)S(1)} %get-tuple-element.17), channel_id=1, replica_groups=mesh['blk'=16,'grp'=2] {'blk'}, dimensions={0}, use_global_device_ids=true | all-gather | bytes 557056 | tf_op jit(solution)/shard_map/all_gather | solution.py:33
  199.2 3.4 fusion.12
  202.6 0.0 copy-done.5
  202.6 40.7 %all-gather.1 = f32[1,1024,128]{2,1,0:T(8,128)S(1)} all-gather(f32[1,64,128]{2,1,0:T(8,128)S(1)} %dynamic-slice_subtract_fusion.6), channel_id=3, replica_groups=mesh['blk'=16,'grp'=2] {'blk'}, dimensions={1}, use_global_device_ids=true | all-gather | bytes 557056 | tf_op jit(solution)/shard_map/all_gather | solution.py:23
  243.3 0.5 bitcast_dynamic-update-slice_fusion.5
  243.8 38.6 %all_gather.48 = f32[1024,128]{1,0:T(8,128)S(1)} all-gather(f32[64,128]{1,0:T(8,128)S(1)} %get-tuple-element.19), channel_id=1, replica_groups=mesh['blk'=16,'grp'=2] {'blk'}, dimensions={0}, use_global_device_ids=true | all-gather | bytes 557056 | tf_op jit(solution)/shard_map/all_gather | solution.py:33
  282.4 3.4 fusion.21
  285.8 40.3 %all-gather.2 = f32[1,1024,128]{2,1,0:T(8,128)S(1)} all-gather(f32[1,64,128]{2,1,0:T(8,128)S(1)} %dynamic-slice_subtract_fusion.5), channel_id=4, replica_groups=mesh['blk'=16,'grp'=2] {'blk'}, dimensions={1}, use_global_device_ids=true | all-gather | bytes 557056 | tf_op jit(solution)/shard_map/all_gather | solution.py:23
  326.1 0.5 bitcast_dynamic-update-slice_fusion.4
  326.6 38.6 %all_gather.50 = f32[1024,128]{1,0:T(8,128)S(1)} all-gather(f32[64,128]{1,0:T(8,128)S(1)} %get-tuple-element.21), channel_id=1, replica_groups=mesh['blk'=16,'grp'=2] {'blk'}, dimensions={0}, use_global_device_ids=true | all-gather | bytes 557056 | tf_op jit(solution)/shard_map/all_gather | solution.py:33
  365.2 3.4 fusion.24
  368.6 41.1 %all-gather.3 = f32[1,1024,128]{2,1,0:T(8,128)S(1)} all-gather(f32[1,64,128]{2,1,0:T(8,128)S(1)} %dynamic-slice_subtract_fusion.4), channel_id=5, replica_groups=mesh['blk'=16,'grp'=2] {'blk'}, dimensions={1}, use_global_device_ids=true | all-gather | bytes 557056 | tf_op jit(solution)/shard_map/all_gather | solution.py:23
  409.8 0.5 bitcast_dynamic-update-slice_fusion.3
  410.2 38.3 %all_gather.52 = f32[1024,128]{1,0:T(8,128)S(1)} all-gather(f32[64,128]{1,0:T(8,128)S(1)} %get-tuple-element.23), channel_id=1, replica_groups=mesh['blk'=16,'grp'=2] {'blk'}, dimensions={0}, use_global_device_ids=true | all-gather | bytes 557056 | tf_op jit(solution)/shard_map/all_gather | solution.py:33
  448.5 0.0 copy-done.1
  448.5 1.8 fusion.27
  450.3 40.8 %all-gather.4 = f32[1,1024,128]{2,1,0:T(8,128)S(1)} all-gather(f32[1,64,128]{2,1,0:T(8,128)S(1)} %dynamic-slice_subtract_fusion.3), channel_id=6, replica_groups=mesh['blk'=16,'grp'=2] {'blk'}, dimensions={1}, use_global_device_ids=true | all-gather | bytes 557056 | tf_op jit(solution)/shard_map/all_gather | solution.py:23
  491.1 0.5 bitcast_dynamic-update-slice_fusion.2
  491.6 38.6 %all_gather.54 = f32[1024,128]{1,0:T(8,128)S(1)} all-gather(f32[64,128]{1,0:T(8,128)S(1)} %get-tuple-element.25), channel_id=1, replica_groups=mesh['blk'=16,'grp'=2] {'blk'}, dimensions={0}, use_global_device_ids=true | all-gather | bytes 557056 | tf_op jit(solution)/shard_map/all_gather | solution.py:33
  530.2 1.8 fusion.30
  532.0 40.5 %all-gather.5 = f32[1,1024,128]{2,1,0:T(8,128)S(1)} all-gather(f32[1,64,128]{2,1,0:T(8,128)S(1)} %dynamic-slice_subtract_fusion.2), channel_id=7, replica_groups=mesh['blk'=16,'grp'=2] {'blk'}, dimensions={1}, use_global_device_ids=true | all-gather | bytes 557056 | tf_op jit(solution)/shard_map/all_gather | solution.py:23
  572.5 0.4 bitcast_dynamic-update-slice_fusion.1
  573.0 38.5 %all_gather.56 = f32[1024,128]{1,0:T(8,128)S(1)} all-gather(f32[64,128]{1,0:T(8,128)S(1)} %get-tuple-element.27), channel_id=1, replica_groups=mesh['blk'=16,'grp'=2] {'blk'}, dimensions={0}, use_global_device_ids=true | all-gather | bytes 557056 | tf_op jit(solution)/shard_map/all_gather | solution.py:33
  611.4 1.8 fusion.33
  613.3 40.4 %all-gather.6 = f32[1,1024,128]{2,1,0:T(8,128)S(1)} all-gather(f32[1,64,128]{2,1,0:T(8,128)S(1)} %dynamic-slice_subtract_fusion.1), channel_id=8, replica_groups=mesh['blk'=16,'grp'=2] {'blk'}, dimensions={1}, use_global_device_ids=true | all-gather | bytes 557056 | tf_op jit(solution)/shard_map/all_gather | solution.py:23
  653.6 0.5 bitcast_dynamic-update-slice_fusion
  654.1 38.3 %all_gather.58 = f32[1024,128]{1,0:T(8,128)S(1)} all-gather(f32[64,128]{1,0:T(8,128)S(1)} %get-tuple-element.29), channel_id=1, replica_groups=mesh['blk'=16,'grp'=2] {'blk'}, dimensions={0}, use_global_device_ids=true | all-gather | bytes 557056 | tf_op jit(solution)/shard_map/all_gather | solution.py:33
  692.4 0.0 copy-start.3
  692.4 0.0 copy-start.4
  692.4 1.8 fusion
  694.2 40.5 %all-gather.7 = f32[1,1024,128]{2,1,0:T(8,128)S(1)} all-gather(f32[1,64,128]{2,1,0:T(8,128)S(1)} %dynamic-slice_subtract_fusion), channel_id=9, replica_groups=mesh['blk'=16,'grp'=2] {'blk'}, dimensions={1}, use_global_device_ids=true | all-gather | bytes 557056 | tf_op jit(solution)/shard_map/all_gather | solution.py:23
  734.7 0.5 fusion.36
  735.2 0.0 copy-done.2
  735.2 0.2 convolution_add_fusion
  735.4 0.0 copy-done.3
  735.4 0.0 copy-done.4
  735.4 1.1 maximum_add_fusion
  (10 shorter events, 0.1 us)
Async XLA Ops:
  7.2 153.0 %copy-start = (f32[8,64,1024]{2,1,0:T(8,128)S(1)}, f32[8,64,1024]{2,1,0:T(8,128)}, u32[]{:S(2)}) copy-start(f32[8,64,1024]{2,1,0:T(8,128)} %param.13) | copy-start | bytes 6291460
  7.2 108.5 %all-reduce.3.cloned.1.call-start = ((), (), s32[]{:S(2)}) async-start(), calls=%async_computation | async-start | bytes 524288 | tf_op jit(solution)/shard_map/psum | solution.py:61
  13.9 43.8 %copy-start.7 = (s32[2,24]{1,0:T(2,128)S(1)}, s32[2,24]{1,0:T(2,128)}, u32[]{:S(2)}) copy-start(s32[2,24]{1,0:T(2,128)} %param.10) | copy-start | bytes 580
  13.9 45.0 %copy-start.6 = (s32[8]{0:T(128)S(1)}, s32[8]{0:T(128)}, u32[]{:S(2)}) copy-start(s32[8]{0:T(128)} %param.11) | copy-start | bytes 100
  57.6 677.5 %copy-start.2 = (f32[2,1024,128]{2,1,0:T(8,128)}, f32[2,1024,128]{2,1,0:T(8,128)S(1)}, u32[]{:S(2)}) copy-start(f32[2,1024,128]{2,1,0:T(8,128)S(1)} %get-tuple-element.5) | copy-start | bytes 3145732
  160.2 42.4 %copy-start.5 = (f32[8,64,128]{2,1,0:T(8,128)S(1)}, f32[8,64,128]{2,1,0:T(8,128)}, u32[]{:S(2)}) copy-start(f32[8,64,128]{2,1,0:T(8,128)} %all-reduce.3.cloned.1.call-done) | copy-start | bytes 786436
  160.2 288.3 %copy-start.1 = (f32[8,8,64,1024]{3,2,1,0:T(8,128)S(1)}, f32[8,8,64,1024]{3,2,1,0:T(8,128)}, u32[]{:S(2)}) copy-start(f32[8,8,64,1024]{3,2,1,0:T(8,128)} %param.12) | copy-start | bytes 50331652
  692.4 43.1 %copy-start.3 = (f32[2,1024,128]{2,1,0:T(8,128)S(1)}, f32[2,1024,128]{2,1,0:T(8,128)}, u32[]{:S(2)}) copy-start(f32[2,1024,128]{2,1,0:T(8,128)} %param.9) | copy-start | bytes 3145732
  692.4 43.1 %copy-start.4 = (f32[2,1000,128]{2,1,0:T(8,128)S(1)}, f32[2,1000,128]{2,1,0:T(8,128)}, u32[]{:S(2)}) copy-start(f32[2,1000,128]{2,1,0:T(8,128)} %slice.42) | copy-start | bytes 3072004
Sparse Core Ops, SparseCore 0:
  59.0 18.0 all-reduce.2
where the time goes:
time: 744 us; the launch traced here: 743 us
  blocking collectives  679 us (91%)
  between operations  29.3 us (4%)
  matrix products  27.4 us (4%)
    all_gather x8, blocking collectives, solve(): lax.all_gather(target, 'blk', axis=0, tiled=True)  328 us
    all_gather x7, blocking collectives, solve(): lax.all_gather(block_value, 'blk', axis=0, tiled=True)  269 us
    psum x2, blocking collectives, squares(): return lax.psum(jnp.sum(residual * residual, axis=(0, 1)), ('blk', 'grp'))  82 us
    dot_general x7, matrix products, solve(): jnp.einsum('aic,cv->aiv', coupling, lax.all_gather(block_value, 'blk', ax...  17.4 us
  transfers between devices with their start and end apart: 1, of which 0 were waited for; matrix products, arithmetic and copies ran while one was open for 0% of the time, Pallas kernels for 0%

commit v1 on v0

--- a/solution.py
+++ b/solution.py
@@ -5,6 +5,22 @@
 
 PANELS = 8
 precise = lax.Precision.HIGHEST
+
+
+def product_in_turn(value, axis, dim, term):
+    count, index, rows = (lax.axis_size(axis), lax.axis_index(axis), value.shape[dim])
+    ahead = [(i, (i + 1) % count) for i in range(count)]
+    downward = [(i, (i - 1) % count) for i in range(count)]
+    half = count // 2
+    from_left = from_right = value
+    subtotal = term(value, index * rows)
+    for step in range(1, half + 1):
+        from_left = lax.ppermute(from_left, axis, ahead)
+        if step < count - half:
+            from_right = lax.ppermute(from_right, axis, downward)
+            subtotal = subtotal + term(from_right, (index + step) % count * rows)
+        subtotal = subtotal + term(from_left, (index - step) % count * rows)
+    return subtotal
 
 
 def squares(residual):
@@ -27,11 +43,16 @@
         solved = lax.dynamic_update_index_in_dim(solved, block_value, current, 0)
         if position + 1 < PANELS:
             coupling = lax.dynamic_index_in_dim(coarse_factor, current, 1, keepdims=False)
-            pending = pending + jnp.einsum(
-                "aic,cv->aiv",
-                coupling,
-                lax.all_gather(block_value, "blk", axis=0, tiled=True),
-                precision=precise,
+            pending = pending + product_in_turn(
+                block_value,
+                "blk",
+                0,
+                lambda own_block, at: jnp.einsum(
+                    "aic,cv->aiv",
+                    lax.dynamic_slice_in_dim(coupling, at, own_block.shape[0], axis=2),
+                    own_block,
+                    precision=precise,
+                ),
             )
     return solved
 

time: 744 us -> 929 us (1.25)
  blocking collectives: 679 us -> 397 us
  starting transfers between devices: 0.04 us -> 254 us
  waiting for transfers between devices: 0.04 us -> 152 us
  matrix products: 27.4 us -> 77.5 us
    all_gather x7 -> x0, blocking collectives: 269 us -> none  [solve(): lax.all_gather(block_value, 'blk', axis=0, tiled=True)]
    ppermute x0 -> x105, starting transfers between devices: none -> 254 us  [the longest x49 246 us: product_in_turn(): from_right = lax.ppermute(from_right, axis, downward)]
    ppermute x0 -> x105, waiting for transfers between devices: none -> 152 us  [the longest x56 143 us: product_in_turn(): from_left = lax.ppermute(from_left, axis, ahead)]
    dot_general x7 -> x112, matrix products: 17.4 us -> 66.8 us  [solve(): jnp.einsum('aic,cv->aiv', lax.dynamic_slice_in_dim(coupling, at, own_bloc...]
    all_gather x8, blocking collectives: 328 us -> 314 us  [solve(): lax.all_gather(target, 'blk', axis=0, tiled=True)]
  transfers between devices with their start and end apart: 1 -> 106, of which waited for: 0 -> 50; matrix products, arithmetic and copies ran while one was open for 0% -> 7% of each run, Pallas kernels for 0% -> 0%
where the time goes in v1:
time: 929 us; the launch traced here: 920 us
  blocking collectives  397 us (43%)
  starting transfers between devices  254 us (27%)
  waiting for transfers between devices  152 us (16%)
  matrix products  77.5 us (8%)
  between operations  31.2 us (3%)
    all_gather x8, blocking collectives, solve(): lax.all_gather(target, 'blk', axis=0, tiled=True)  314 us
    ppermute x49, starting transfers between devices, product_in_turn(): from_right = lax.ppermute(from_right, axis, downward)  246 us
    ppermute x56, waiting for transfers between devices, product_in_turn(): from_left = lax.ppermute(from_left, axis, ahead)  143 us
    psum x2, blocking collectives, squares(): return lax.psum(jnp.sum(residual * residual, axis=(0, 1)), ('blk', 'grp'))  82 us
    dot_general x112, matrix products, solve(): jnp.einsum('aic,cv->aiv', lax.dynamic_slice_in_dim(coupling, at, own_bloc...  66.8 us
  transfers between devices with their start and end apart: 106, of which 50 were waited for; matrix products, arithmetic and copies ran while one was open for 7% of the time, Pallas kernels for 0%

profile of v1, /device:TPU:0, one launch (start us, length us, event | category | flops | bytes accessed | tf_op | source)
XLA Modules:
  0.0 919.6 jit_solution(7226736238444284259)
XLA Ops:
  13.9 41.9 %all-reduce = (f32[128]{0:T(128)S(1)}, f32[128]{0:T(128)S(1)}) all-reduce(f32[128]{0:T(128)S(1)} %multiply_reduce_fusion.2, f32[128]{0:T(128)S(1)} %get-tuple-element.14), channel_id=1, replica_groups=mesh['blk'=16,'grp'=2] {'blk','grp'}, use_global_device_ids=true, to_apply=%region_1.0 | all-reduce | flops 256 | bytes 2048 | tf_op jit(solution)/shard_map/psum | solution.py:27
  76.7 40.1 %psum.31 = f32[128]{0:T(128)S(1)} all-reduce(f32[128]{0:T(128)S(1)} %get-tuple-element.4), channel_id=1, replica_groups=mesh['blk'=16,'grp'=2] {'blk','grp'}, use_global_device_ids=true, to_apply=%region_6.0 | all-reduce | flops 128 | bytes 1024 | tf_op jit(solution)/shard_map/psum | solution.py:27
  118.4 43.9 %all-gather = f32[1,1024,128]{2,1,0:T(8,128)S(1)} all-gather(f32[1,64,128]{2,1,0:T(8,128)S(1)} %constant_dynamic-slice_fusion.19), channel_id=2, replica_groups=mesh['blk'=16,'grp'=2] {'blk'}, dimensions={1}, use_global_device_ids=true | all-gather | bytes 557056 | tf_op jit(solution)/shard_map/all_gather | solution.py:39
  170.4 5.6 collective-permute-start.2
  180.4 5.7 collective-permute-start.4
  189.2 5.6 collective-permute-start.6
  197.9 5.6 collective-permute-start.8
  206.6 5.6 collective-permute-start.10
  215.3 5.6 collective-permute-start.12
  232.4 39.9 %all-gather.1 = f32[1,1024,128]{2,1,0:T(8,128)S(1)} all-gather(f32[1,64,128]{2,1,0:T(8,128)S(1)} %fusion.477), channel_id=3, replica_groups=mesh['blk'=16,'grp'=2] {'blk'}, dimensions={1}, use_global_device_ids=true | all-gather | bytes 557056 | tf_op jit(solution)/shard_map/all_gather | solution.py:39
  283.0 7.1 collective-permute-done.18
  290.7 5.6 collective-permute-start.19
  298.7 5.6 collective-permute-start.21
  306.7 5.6 collective-permute-start.23
  314.8 5.6 collective-permute-start.25
  323.1 5.6 collective-permute-start.27
  331.8 7.4 collective-permute-done.29
  339.7 38.5 %all-gather.2 = f32[1,1024,128]{2,1,0:T(8,128)S(1)} all-gather(f32[1,64,128]{2,1,0:T(8,128)S(1)} %fusion.478), channel_id=4, replica_groups=mesh['blk'=16,'grp'=2] {'blk'}, dimensions={1}, use_global_device_ids=true | all-gather | bytes 557056 | tf_op jit(solution)/shard_map/all_gather | solution.py:39
  382.8 5.9 collective-permute-start.32
  389.6 7.4 collective-permute-done.33
  397.5 5.8 collective-permute-start.34
  405.5 5.6 collective-permute-start.36
  413.5 5.6 collective-permute-start.38
  421.5 5.6 collective-permute-start.40
  429.9 5.6 collective-permute-start.42
  438.3 7.0 collective-permute-done.44
  445.8 38.6 %all-gather.3 = f32[1,1024,128]{2,1,0:T(8,128)S(1)} all-gather(f32[1,64,128]{2,1,0:T(8,128)S(1)} %fusion.479), channel_id=5, replica_groups=mesh['blk'=16,'grp'=2] {'blk'}, dimensions={1}, use_global_device_ids=true | all-gather | bytes 557056 | tf_op jit(solution)/shard_map/all_gather | solution.py:39
  488.8 5.8 collective-permute-start.47
  495.6 7.3 collective-permute-done.48
  503.4 5.6 collective-permute-start.49
  511.4 5.6 collective-permute-start.51
  519.6 5.6 collective-permute-start.53
  527.6 5.6 collective-permute-start.55
  535.6 5.6 collective-permute-start.57
  544.5 7.0 collective-permute-done.59
  552.0 38.5 %all-gather.4 = f32[1,1024,128]{2,1,0:T(8,128)S(1)} all-gather(f32[1,64,128]{2,1,0:T(8,128)S(1)} %fusion.480), channel_id=6, replica_groups=mesh['blk'=16,'grp'=2] {'blk'}, dimensions={1}, use_global_device_ids=true | all-gather | bytes 557056 | tf_op jit(solution)/shard_map/all_gather | solution.py:39
  595.0 5.7 collective-permute-start.62
  601.6 7.2 collective-permute-done.63
  609.4 5.6 collective-permute-start.64
  617.4 5.6 collective-permute-start.66
  625.4 5.6 collective-permute-start.68
  633.4 5.6 collective-permute-start.70
  641.5 5.6 collective-permute-start.72
  649.9 7.0 collective-permute-done.74
  657.4 38.4 %all-gather.5 = f32[1,1024,128]{2,1,0:T(8,128)S(1)} all-gather(f32[1,64,128]{2,1,0:T(8,128)S(1)} %fusion.481), channel_id=7, replica_groups=mesh['blk'=16,'grp'=2] {'blk'}, dimensions={1}, use_global_device_ids=true | all-gather | bytes 557056 | tf_op jit(solution)/shard_map/all_gather | solution.py:39
  700.2 5.5 collective-permute-start.77
  706.7 7.1 collective-permute-done.78
  714.3 5.6 collective-permute-start.79
  722.3 5.8 collective-permute-start.81
  730.3 5.6 collective-permute-start.83
  738.3 5.6 collective-permute-start.85
  746.3 5.6 collective-permute-start.87
  754.8 7.0 collective-permute-done.89
  762.3 38.5 %all-gather.6 = f32[1,1024,128]{2,1,0:T(8,128)S(1)} all-gather(f32[1,64,128]{2,1,0:T(8,128)S(1)} %fusion.482), channel_id=8, replica_groups=mesh['blk'=16,'grp'=2] {'blk'}, dimensions={1}, use_global_device_ids=true | all-gather | bytes 557056 | tf_op jit(solution)/shard_map/all_gather | solution.py:39
  805.2 5.5 collective-permute-start.92
  811.7 7.2 collective-permute-done.93
  819.4 5.6 collective-permute-start.94
  827.4 5.6 collective-permute-start.96
  835.4 5.6 collective-permute-start.98
  843.4 5.6 collective-permute-start.100
  850.6 5.9 collective-permute-start.102
  857.5 7.1 collective-permute-done.103
  865.4 6.6 collective-permute-done.104
  872.5 38.3 %all-gather.7 = f32[1,1024,128]{2,1,0:T(8,128)S(1)} all-gather(f32[1,64,128]{2,1,0:T(8,128)S(1)} %fusion.484), channel_id=9, replica_groups=mesh['blk'=16,'grp'=2] {'blk'}, dimensions={1}, use_global_device_ids=true | all-gather | bytes 557056 | tf_op jit(solution)/shard_map/all_gather | solution.py:39
  (312 shorter events, 168.3 us)
Async XLA Ops:
  7.2 110.3 %all-reduce.3.cloned.1.call-start = ((), (), s32[]{:S(2)}) async-start(), calls=%async_computation | async-start | bytes 524288 | tf_op jit(solution)/shard_map/psum | solution.py:82
  170.4 8.5 collective-permute-start.3
  170.4 10.0 %collective-permute-start.2 = (f32[64,128]{1,0:T(8,128)S(1)}, f32[64,128]{1,0:T(8,128)S(1)}, u32[]{:S(2)}, u32[]{:S(2)}) collective-permute-start(f32[64,128]{1,0:T(8,128)S(1)} %collective-permute-done), channel_id=1, source_target_pairs={{0,30},{2,0},{4,2},{6,4},{8,6},{10,8},{12,10},{14,12},{16,14},{18,... | collective-permute-start | bytes 98312 | tf_op jit(solution)/shard_map/ppermute | solution.py:20
  178.9 8.7 collective-permute-start.5
  180.4 8.8 collective-permute-start.4
  187.6 8.7 collective-permute-start.7
  189.2 8.7 collective-permute-start.6
  196.3 8.7 collective-permute-start.9
  197.9 8.7 collective-permute-start.8
  205.0 8.7 collective-permute-start.11
  206.6 8.7 collective-permute-start.10
  213.7 8.7 collective-permute-start.13
  215.3 8.9 collective-permute-start.12
  273.5 9.0 collective-permute-start.16
  276.8 13.9 %collective-permute-start.17 = (f32[64,128]{1,0:T(8,128)S(1)}, f32[64,128]{1,0:T(8,128)S(1)}, u32[]{:S(2)}, u32[]{:S(2)}) collective-permute-start(f32[64,128]{1,0:T(8,128)S(1)} %collective-permute-done.15), channel_id=1, source_target_pairs={{0,30},{2,0},{4,2},{6,4},{8,6},{10,8},{12,10},{14,12},{16,14},{18,... | collective-permute-start | bytes 98312 | tf_op jit(solution)/shard_map/ppermute | solution.py:20
  290.7 8.0 collective-permute-start.19
  298.7 8.0 collective-permute-start.21
  306.7 8.1 collective-permute-start.23
  314.7 7.9 collective-permute-start.26
  314.8 8.3 collective-permute-start.25
  323.0 7.9 collective-permute-start.28
  323.1 8.3 collective-permute-start.27
  331.3 7.9 collective-permute-start.29
  380.9 8.2 collective-permute-start.31
  382.8 14.7 %collective-permute-start.32 = (f32[64,128]{1,0:T(8,128)S(1)}, f32[64,128]{1,0:T(8,128)S(1)}, u32[]{:S(2)}, u32[]{:S(2)}) collective-permute-start(f32[64,128]{1,0:T(8,128)S(1)} %collective-permute-done.30), channel_id=1, source_target_pairs={{0,30},{2,0},{4,2},{6,4},{8,6},{10,8},{12,10},{14,12},{16,14},{18,... | collective-permute-start | bytes 98312 | tf_op jit(solution)/shard_map/ppermute | solution.py:20
  389.1 7.9 collective-permute-start.33
  397.5 8.0 collective-permute-start.34
  405.5 8.0 collective-permute-start.36
  413.5 8.1 collective-permute-start.38
  421.5 7.9 collective-permute-start.41
  421.5 8.3 collective-permute-start.40
  429.9 8.0 collective-permute-start.42
  486.8 8.2 collective-permute-start.46
  488.8 14.5 %collective-permute-start.47 = (f32[64,128]{1,0:T(8,128)S(1)}, f32[64,128]{1,0:T(8,128)S(1)}, u32[]{:S(2)}, u32[]{:S(2)}) collective-permute-start(f32[64,128]{1,0:T(8,128)S(1)} %collective-permute-done.45), channel_id=1, source_target_pairs={{0,30},{2,0},{4,2},{6,4},{8,6},{10,8},{12,10},{14,12},{16,14},{18,... | collective-permute-start | bytes 98312 | tf_op jit(solution)/shard_map/ppermute | solution.py:20
  495.1 7.8 collective-permute-start.48
  503.4 8.0 collective-permute-start.49
  511.3 7.8 collective-permute-start.52
  511.4 8.3 collective-permute-start.51
  519.6 8.0 collective-permute-start.53
  527.6 8.0 collective-permute-start.55
  535.6 8.4 collective-permute-start.57
  543.6 8.0 collective-permute-start.59
  593.1 8.0 collective-permute-start.61
  595.0 14.4 %collective-permute-start.62 = (f32[64,128]{1,0:T(8,128)S(1)}, f32[64,128]{1,0:T(8,128)S(1)}, u32[]{:S(2)}, u32[]{:S(2)}) collective-permute-start(f32[64,128]{1,0:T(8,128)S(1)} %collective-permute-done.60), channel_id=1, source_target_pairs={{0,30},{2,0},{4,2},{6,4},{8,6},{10,8},{12,10},{14,12},{16,14},{18,... | collective-permute-start | bytes 98312 | tf_op jit(solution)/shard_map/ppermute | solution.py:20
  601.1 7.8 collective-permute-start.63
  609.4 8.0 collective-permute-start.64
  617.4 8.0 collective-permute-start.66
  625.4 8.0 collective-permute-start.68
  633.4 8.0 collective-permute-start.70
  641.5 8.0 collective-permute-start.72
  698.2 8.0 collective-permute-start.76
  700.2 14.1 %collective-permute-start.77 = (f32[64,128]{1,0:T(8,128)S(1)}, f32[64,128]{1,0:T(8,128)S(1)}, u32[]{:S(2)}, u32[]{:S(2)}) collective-permute-start(f32[64,128]{1,0:T(8,128)S(1)} %collective-permute-done.75), channel_id=1, source_target_pairs={{0,30},{2,0},{4,2},{6,4},{8,6},{10,8},{12,10},{14,12},{16,14},{18,... | collective-permute-start | bytes 98312 | tf_op jit(solution)/shard_map/ppermute | solution.py:20
  714.3 8.0 collective-permute-start.79
  722.3 8.0 collective-permute-start.81
  730.3 8.0 collective-permute-start.83
  738.3 8.0 collective-permute-start.85
  746.3 8.1 collective-permute-start.87
  803.2 8.0 collective-permute-start.91
  805.2 14.2 %collective-permute-start.92 = (f32[64,128]{1,0:T(8,128)S(1)}, f32[64,128]{1,0:T(8,128)S(1)}, u32[]{:S(2)}, u32[]{:S(2)}) collective-permute-start(f32[64,128]{1,0:T(8,128)S(1)} %collective-permute-done.90), channel_id=1, source_target_pairs={{0,30},{2,0},{4,2},{6,4},{8,6},{10,8},{12,10},{14,12},{16,14},{18,... | collective-permute-start | bytes 98312 | tf_op jit(solution)/shard_map/ppermute | solution.py:20
  819.4 8.0 collective-permute-start.94
  827.4 8.0 collective-permute-start.96
  835.4 8.0 collective-permute-start.98
  843.3 13.6 %collective-permute-start.101 = (f32[64,128]{1,0:T(8,128)S(1)}, f32[64,128]{1,0:T(8,128)S(1)}, u32[]{:S(2)}, u32[]{:S(2)}) collective-permute-start(f32[64,128]{1,0:T(8,128)S(1)} %collective-permute-done.99), channel_id=1, source_target_pairs={{0,2},{2,4},{4,6},{6,8},{8,10},{10,12},{12,14},{14,16},{16,18},{18... | collective-permute-start | bytes 98312 | tf_op jit(solution)/shard_map/ppermute | solution.py:18
  850.6 14.4 %collective-permute-start.102 = (f32[64,128]{1,0:T(8,128)S(1)}, f32[64,128]{1,0:T(8,128)S(1)}, u32[]{:S(2)}, u32[]{:S(2)}) collective-permute-start(f32[64,128]{1,0:T(8,128)S(1)} %collective-permute-done.100), channel_id=1, source_target_pairs={{0,30},{2,0},{4,2},{6,4},{8,6},{10,8},{12,10},{14,12},{16,14},{18,... | collective-permute-start | bytes 98312 | tf_op jit(solution)/shard_map/ppermute | solution.py:20
  (49 other events, 2502.9 us)
Sparse Core Ops, SparseCore 0:
  59.7 18.0 all-reduce.2
